TPU v7x, 128 devices: a whole 4x4x4 slice. The times are simulated.
128 devices in a mesh: smp: 32 (over x, z, y_lo), col: 2 (over core), slab: 2 (over y_hi).
Axes of the slice: x: 4, y: 4 (y_hi: 2, y_lo: 2; y = y_hi * 2 + y_lo), z: 4, core: 2. Of those that a mesh axis runs over, the one named last changes fastest.
Arguments:
- jacobian: bfloat16 [1024, 32, 16384], P('smp', 'slab', 'col'), may hold values from -0.005722046 to 0.005722046
- local_energy: float32 [1024], P('smp'), may hold values from -6 to 6
Outputs:
- update: float32 [32, 16384], P('slab', ('col', 'smp'))
All inputs are finite; a program needn't handle non-finite values.
Results may differ from a plain program's by a relative error of at most 0.0085.
Values may be sent and summed in bfloat16 or wider, within the bound.
A program may use at most 192 MiB of HBM per device.

v0:
```python
import jax
import jax.numpy as jnp
from jax import lax
from jax.sharding import PartitionSpec as P

SLABS = 32
SLAB_COLS = 16384


def shards(jacobian, local_energy):
    energies = lax.all_gather(local_energy, "smp", axis=0, tiled=True)
    jacobian, energies = lax.optimization_barrier((jacobian, energies))
    samples = energies.shape[0]
    root_count = jnp.sqrt(jnp.float32(samples))
    eps = (energies - jnp.mean(energies)) / root_count
    columns = lax.all_to_all(jacobian, "smp", split_axis=2, concat_axis=0, tiled=True)
    slab_count = columns.shape[1]
    width = columns.shape[2]
    values = columns.astype(jnp.float32)
    mean_row = jnp.mean(values, axis=0, keepdims=True)
    centered = (
        ((values - mean_row) / root_count).astype(jnp.bfloat16).reshape(samples, slab_count * width)
    )
    partial_gram = jnp.dot(centered, centered.T, preferred_element_type=jnp.float32)
    gram = lax.psum(partial_gram, ("smp", "col", "slab"))
    shift = 0.01 * jnp.trace(gram) / samples
    factor = jnp.linalg.cholesky(gram + shift * jnp.eye(samples, dtype=jnp.float32))
    middle = lax.linalg.triangular_solve(factor, eps[:, None], left_side=True, lower=True)
    coeffs = lax.linalg.triangular_solve(
        factor, middle, left_side=True, lower=True, transpose_a=True
    )[:, 0]
    delta = jnp.dot(coeffs, centered.astype(jnp.float32), precision=lax.Precision.HIGHEST)
    squared = jnp.dot(
        coeffs,
        jnp.dot(gram, coeffs, precision=lax.Precision.HIGHEST),
        precision=lax.Precision.HIGHEST,
    )
    limit = 0.3 * jnp.sqrt(jnp.float32(SLABS * SLAB_COLS))
    scaled = -jnp.minimum(1.0, limit / jnp.sqrt(squared)) * delta
    return scaled.reshape(slab_count, width)


def solution(mesh):
    in_specs = (P("smp", "slab", "col"), P("smp"))
    out_specs = P("slab", ("col", "smp"))
    return jax.shard_map(shards, mesh=mesh, in_specs=in_specs, out_specs=out_specs, check_vma=False)
```

profile of v0, /device:TPU:1, one launch (start us, length us, event | category | flops | bytes accessed | tf_op | source)
XLA Modules:
  0.0 905.1 jit_solution(12480278940735346125)
XLA Ops:
  9.3 70.8 %all-reduce.1 = f32[1024]{0:T(1024)S(1)} all-reduce(f32[1024]{0:T(1024)S(1)} %dynamic-update-slice.47), channel_id=1, replica_groups=mesh['smp'=32,'col'=2,'slab'=2] {'smp'}, use_global_device_ids=true, to_apply=%add.1 | all-reduce | flops 1024 | bytes 8192 | tf_op jit(solution)/shard_map/optimization_barrier | solution.py:12
  80.1 45.6 %copy.65 = bf16[32,16,8192]{0,1,2:T(8,128)(2,1)} copy(bf16[32,16,8192]{2,1,0:T(8,128)(2,1)} %param.2) | data formatting | bytes 16777216 | tf_op jit(solution)/shard_map/optimization_barrier | solution.py:12
  125.7 39.8 %reshape.346 = bf16[32,2,65536]{2,1,0:T(2,128)(2,1)} reshape(bf16[8192,16,32]{2,1,0:T(8,128)(2,1)} %bitcast.343) | data formatting | bytes 16777216
  165.5 86.4 %all_to_all.4 = bf16[32,2,65536]{2,1,0:T(2,128)(2,1)} all-to-all(bf16[32,2,65536]{2,1,0:T(2,128)(2,1)} %reshape.346), channel_id=1, replica_groups=mesh['smp'=32,'col'=2,'slab'=2] {'smp'}, dimensions={0} | all-to-all | bytes 16777216 | tf_op jit(solution)/shard_map/all_to_all | solution.py:16
  251.9 30.6 %reshape.347 = bf16[8192,16,32]{2,1,0:T(8,128)(2,1)} reshape(bf16[32,2,65536]{2,1,0:T(2,128)(2,1)} %all_to_all.4) | data formatting | bytes 16777216
  282.5 44.0 %copy.66 = f32[32,16,32,256]{3,1,0,2:T(8,128)} copy(bf16[32,16,32,256]{0,1,3,2:T(8,128)(2,1)} %bitcast.342) | data formatting | bytes 25165824 | tf_op jit(solution)/shard_map/convert_element_type | solution.py:19
  326.6 6.9 bitcast_reduce_fusion
  333.5 7.2 fusion.1
  340.6 3.2 copy-done.1
  343.8 16.8 %fusion.5 = f32[1024,1024]{0,1:T(8,128)} fusion(bf16[1024,16,256]{2,1,0:T(8,128)(2,1)S(1)} %bitcast.345), kind=kOutput, calls=%fused_computation.15 | convolution fusion | flops 8589934592 | bytes 12582912 | tf_op jit(solution)/shard_map/dot_general | solution.py:24
  362.1 12.2 %copy.98 = bf16[128,8,16,256]{3,1,2,0:T(8,128)(2,1)} copy(bf16[128,8,16,256]{3,2,1,0:T(8,128)(2,1)} %bitcast.346) | data formatting | bytes 16777216
  374.3 155.4 %all-reduce.4.cloned.1.call-done = f32[1024,1024]{0,1:T(8,128)} async-done(((f32[1024,1024]{0,1:T(8,128)}), f32[1024,1024]{0,1:T(8,128)}) %all-reduce.4.cloned.1.call-update) | async-done | bytes 4194320 | tf_op jit(solution)/shard_map/psum | solution.py:25
  529.7 2.9 select_reduce_fusion
  533.2 4.8 select_add_fusion
  538.0 5.7 copy.70
  543.8 4.5 fusion.4
  550.2 11.7 %cholesky.222 = f32[128,128]{1,0:T(8,128)S(1)} custom-call(f32[128,128]{1,0:T(8,128)S(1)} %cholesky.577), custom_call_target="Cholesky" | custom-call | tf_op jit(solution)/shard_map/jit(cholesky)/cholesky | solution.py:27
  562.0 9.8 %custom-call.64 = f32[1,128,128]{1,2,0:T(8,128)S(1)} custom-call(f32[1,128,128]{2,1,0:T(8,128)S(1)} %get-tuple-element.56), custom_call_target="InvertDiagBlocksLowerTriangular" | custom-call | tf_op jit(solution)/shard_map/jit(cholesky)/cholesky | solution.py:27
  574.9 11.7 %cholesky.243 = f32[128,128]{1,0:T(8,128)S(1)} custom-call(f32[128,128]{1,0:T(8,128)S(1)} %cholesky.581), custom_call_target="Cholesky" | custom-call | tf_op jit(solution)/shard_map/jit(cholesky)/cholesky | solution.py:27
  587.2 2.5 cholesky.254
  589.7 9.8 %custom-call.65 = f32[1,128,128]{1,2,0:T(8,128)S(1)} custom-call(f32[1,128,128]{2,1,0:T(8,128)S(1)} %get-tuple-element.54), custom_call_target="InvertDiagBlocksLowerTriangular" | custom-call | tf_op jit(solution)/shard_map/jit(cholesky)/cholesky | solution.py:27
  602.3 2.7 convolution_subtract_fusion.1
  605.1 11.7 %cholesky.466 = f32[128,128]{1,0:T(8,128)S(1)} custom-call(f32[128,128]{1,0:T(8,128)S(1)} %cholesky.586), custom_call_target="Cholesky" | custom-call | tf_op jit(solution)/shard_map/jit(cholesky)/cholesky | solution.py:27
  617.6 9.8 %custom-call.66 = f32[1,128,128]{1,2,0:T(8,128)S(1)} custom-call(f32[1,128,128]{2,1,0:T(8,128)S(1)} %get-tuple-element.52), custom_call_target="InvertDiagBlocksLowerTriangular" | custom-call | tf_op jit(solution)/shard_map/jit(cholesky)/cholesky | solution.py:27
  628.6 3.3 convolution_subtract_fusion.2
  632.0 11.7 %cholesky.485 = f32[128,128]{1,0:T(8,128)S(1)} custom-call(f32[128,128]{1,0:T(8,128)S(1)} %cholesky.591), custom_call_target="Cholesky" | custom-call | tf_op jit(solution)/shard_map/jit(cholesky)/cholesky | solution.py:27
  644.5 9.8 %custom-call.67 = f32[1,128,128]{1,2,0:T(8,128)S(1)} custom-call(f32[1,128,128]{2,1,0:T(8,128)S(1)} %get-tuple-element.50), custom_call_target="InvertDiagBlocksLowerTriangular" | custom-call | tf_op jit(solution)/shard_map/jit(cholesky)/cholesky | solution.py:27
  655.4 3.2 convolution_subtract_fusion.3
  658.6 12.1 %cholesky.504 = f32[128,128]{1,0:T(8,128)S(1)} custom-call(f32[128,128]{1,0:T(8,128)S(1)} %cholesky.596), custom_call_target="Cholesky" | custom-call | tf_op jit(solution)/shard_map/jit(cholesky)/cholesky | solution.py:27
  671.4 9.8 %custom-call.68 = f32[1,128,128]{1,2,0:T(8,128)S(1)} custom-call(f32[1,128,128]{2,1,0:T(8,128)S(1)} %get-tuple-element.48), custom_call_target="InvertDiagBlocksLowerTriangular" | custom-call | tf_op jit(solution)/shard_map/jit(cholesky)/cholesky | solution.py:27
  682.4 3.1 convolution_subtract_fusion.4
  685.5 11.7 %cholesky.524 = f32[128,128]{1,0:T(8,128)S(1)} custom-call(f32[128,128]{1,0:T(8,128)S(1)} %cholesky.601), custom_call_target="Cholesky" | custom-call | tf_op jit(solution)/shard_map/jit(cholesky)/cholesky | solution.py:27
  698.0 9.8 %custom-call.69 = f32[1,128,128]{1,2,0:T(8,128)S(1)} custom-call(f32[1,128,128]{2,1,0:T(8,128)S(1)} %get-tuple-element.46), custom_call_target="InvertDiagBlocksLowerTriangular" | custom-call | tf_op jit(solution)/shard_map/jit(cholesky)/cholesky | solution.py:27
  708.8 2.8 convolution_subtract_fusion.5
  711.6 11.7 %cholesky.544 = f32[128,128]{1,0:T(8,128)S(1)} custom-call(f32[128,128]{1,0:T(8,128)S(1)} %cholesky.606), custom_call_target="Cholesky" | custom-call | tf_op jit(solution)/shard_map/jit(cholesky)/cholesky | solution.py:27
  724.1 9.8 %custom-call.70 = f32[1,128,128]{1,2,0:T(8,128)S(1)} custom-call(f32[1,128,128]{2,1,0:T(8,128)S(1)} %get-tuple-element.44), custom_call_target="InvertDiagBlocksLowerTriangular" | custom-call | tf_op jit(solution)/shard_map/jit(cholesky)/cholesky | solution.py:27
  736.9 11.7 %cholesky.562 = f32[128,128]{1,0:T(8,128)S(1)} custom-call(f32[128,128]{1,0:T(8,128)S(1)} %convolution_subtract_fusion.6), custom_call_target="Cholesky" | custom-call | tf_op jit(solution)/shard_map/jit(cholesky)/cholesky | solution.py:27
  758.8 4.9 select_select_fusion
  763.7 24.5 %while.1 = (s32[]{:T(128)}, f32[1024,1024]{0,1:T(8,128)}, s32[8,2]{0,1:T(2,128)S(1)}, f32[8,128,128]{2,1,0:T(8,128)S(1)}, s32[]{:T(128)}) while((s32[]{:T(128)}, f32[1024,1024]{0,1:T(8,128)}, s32[8,2]{0,1:T(2,128)S(1)}, f32[8,128,128]{2,1,0:T(8,128)S(1)}, s32[]{:T(128)}) %tuple.54), condition=%wide.while_cond, body=%wide.while_body.sunk | while | flops 2 | bytes 393321 | solution.py:29
  764.3 2.3 dynamic-slice.8
  767.4 2.3 dynamic-slice.8
  770.5 2.3 dynamic-slice.8
  773.5 2.3 dynamic-slice.8
  776.6 2.3 dynamic-slice.8
  779.7 2.3 dynamic-slice.8
  788.2 78.8 %custom-call.71 = f32[8,128,128]{1,2,0:T(8,128)S(1)} custom-call(f32[8,128,128]{2,1,0:T(8,128)S(1)} %get-tuple-element.16), custom_call_target="InvertDiagBlocksLowerTriangular" | custom-call | tf_op jit(solution)/shard_map/triangular_solve | solution.py:29
  888.1 2.3 fusion.125
  891.7 5.7 fusion.126
  (153 shorter events, 60.8 us)
Async XLA Ops:
  6.5 523.2 %all-reduce.4.cloned.1.call-start = ((), (), s32[]{:S(2)}) async-start(), calls=%async_computation.1 | async-start | bytes 8388608 | tf_op jit(solution)/shard_map/psum | solution.py:25
  340.6 3.2 copy-start.1
  548.3 2.0 copy-start.2
  867.0 21.1 %copy-start = (f32[1024,1024]{0,1:T(8,128)S(1)}, f32[1024,1024]{0,1:T(8,128)}, u32[]{:S(2)}) copy-start(f32[1024,1024]{0,1:T(8,128)} %all-reduce.4.cloned.1.call-done) | copy-start | bytes 12582916
Sparse Core Ops, SparseCore 0:
  360.8 168.8 all-reduce.3
where the time goes:
time: 912 us; the launch traced here: 905 us
  other arithmetic  279 us (31%)
  local copies, waits for them, and re-layouts  219 us (24%)
  blocking collectives  157 us (17%)
  waiting for transfers between devices  155 us (17%)
  matrix products  72.4 us (8%)
  between operations  21.5 us (2%)
    another operation x30, other arithmetic, shards(): jnp.linalg.cholesky(gram + shift * jnp.eye(samples, dtype=jnp.float32))  168 us
    psum x1, waiting for transfers between devices, shards(): gram = lax.psum(partial_gram, ('smp', 'col', 'slab'))  155 us
    unnamed x30, local copies, waits for them, and re-layouts  90.2 us
    all_to_all x1, blocking collectives, shards(): lax.all_to_all(jacobian, 'smp', split_axis=2, concat_axis=0, tiled=True)  86.4 us
    another operation x3, other arithmetic, shards(): lax.linalg.triangular_solve(factor, middle, left_side=True, lower=True, t...  83.7 us
    optimization_barrier x1, blocking collectives, shards(): jacobian, energies = lax.optimization_barrier((jacobian, energies))  70.8 us
    optimization_barrier x1, local copies, waits for them, and re-layouts, shards(): jacobian, energies = lax.optimization_barrier((jacobian, energies))  45.6 us
    convert_element_type x1, local copies, waits for them, and re-layouts, shards(): values = columns.astype(jnp.float32)  44 us
  transfers between devices with their start and end apart: 1, of which 1 were waited for; matrix products, arithmetic and copies ran while one was open for 1% of the time, Pallas kernels for 0%

commit v1 on v0

--- a/solution.py
+++ b/solution.py
@@ -22,7 +22,7 @@
         ((values - mean_row) / root_count).astype(jnp.bfloat16).reshape(samples, slab_count * width)
     )
     partial_gram = jnp.dot(centered, centered.T, preferred_element_type=jnp.float32)
-    gram = lax.psum(partial_gram, ("smp", "col", "slab"))
+    gram = lax.psum(lax.psum(partial_gram, "smp"), ("col", "slab"))
     shift = 0.01 * jnp.trace(gram) / samples
     factor = jnp.linalg.cholesky(gram + shift * jnp.eye(samples, dtype=jnp.float32))
     middle = lax.linalg.triangular_solve(factor, eps[:, None], left_side=True, lower=True)

time: 912 us -> 1240 us (1.36)
  waiting for transfers between devices: 155 us -> 487 us
    psum x1 -> x2, waiting for transfers between devices: 155 us -> 487 us  [shards(): gram = lax.psum(lax.psum(partial_gram, 'smp'), ('col', 'slab'))]
  transfers between devices with their start and end apart: 1 -> 2, of which waited for: 1 -> 2; matrix products, arithmetic and copies ran while one was open for 1% -> 1% of each run, Pallas kernels for 0% -> 0%
where the time goes in v1:
time: 1240 us
  waiting for transfers between devices  487 us (39%)
  other arithmetic  279 us (22%)
  local copies, waits for them, and re-layouts  219 us (18%)
  blocking collectives  157 us (13%)
  matrix products  72.2 us (6%)
  between operations  21.6 us (2%)
    psum x2, waiting for transfers between devices, shards(): gram = lax.psum(lax.psum(partial_gram, 'smp'), ('col', 'slab'))  487 us
    another operation x30, other arithmetic, shards(): jnp.linalg.cholesky(gram + shift * jnp.eye(samples, dtype=jnp.float32))  168 us
    unnamed x30, local copies, waits for them, and re-layouts  90.2 us
    all_to_all x1, blocking collectives, shards(): lax.all_to_all(jacobian, 'smp', split_axis=2, concat_axis=0, tiled=True)  86.4 us
    another operation x3, other arithmetic, shards(): lax.linalg.triangular_solve(factor, middle, left_side=True, lower=True, t...  83.7 us
    optimization_barrier x1, blocking collectives, shards(): jacobian, energies = lax.optimization_barrier((jacobian, energies))  70.8 us
    optimization_barrier x1, local copies, waits for them, and re-layouts, shards(): jacobian, energies = lax.optimization_barrier((jacobian, energies))  45.6 us
    convert_element_type x1, local copies, waits for them, and re-layouts, shards(): values = columns.astype(jnp.float32)  44 us
  transfers between devices with their start and end apart: 2, of which 2 were waited for; matrix products, arithmetic and copies ran while one was open for 1% of the time, Pallas kernels for 0%

profile of v1, /device:TPU:1, one launch (start us, length us, event | category | flops | bytes accessed | tf_op | source)
XLA Modules:
  0.0 1237.2 jit_solution(16327585318854223962)
XLA Ops:
  9.3 70.8 %all-reduce.1 = f32[1024]{0:T(1024)S(1)} all-reduce(f32[1024]{0:T(1024)S(1)} %dynamic-update-slice.47), channel_id=1, replica_groups=mesh['smp'=32,'col'=2,'slab'=2] {'smp'}, use_global_device_ids=true, to_apply=%add.1 | all-reduce | flops 1024 | bytes 8192 | tf_op jit(solution)/shard_map/optimization_barrier | solution.py:12
  80.1 45.6 %copy.65 = bf16[32,16,8192]{0,1,2:T(8,128)(2,1)} copy(bf16[32,16,8192]{2,1,0:T(8,128)(2,1)} %param.2) | data formatting | bytes 16777216 | tf_op jit(solution)/shard_map/optimization_barrier | solution.py:12
  125.7 39.8 %reshape.346 = bf16[32,2,65536]{2,1,0:T(2,128)(2,1)} reshape(bf16[8192,16,32]{2,1,0:T(8,128)(2,1)} %bitcast.343) | data formatting | bytes 16777216
  165.5 86.4 %all_to_all.4 = bf16[32,2,65536]{2,1,0:T(2,128)(2,1)} all-to-all(bf16[32,2,65536]{2,1,0:T(2,128)(2,1)} %reshape.346), channel_id=1, replica_groups=mesh['smp'=32,'col'=2,'slab'=2] {'smp'}, dimensions={0} | all-to-all | bytes 16777216 | tf_op jit(solution)/shard_map/all_to_all | solution.py:16
  251.9 30.6 %reshape.347 = bf16[8192,16,32]{2,1,0:T(8,128)(2,1)} reshape(bf16[32,2,65536]{2,1,0:T(2,128)(2,1)} %all_to_all.4) | data formatting | bytes 16777216
  282.5 44.0 %copy.66 = f32[32,16,32,256]{3,1,0,2:T(8,128)} copy(bf16[32,16,32,256]{0,1,3,2:T(8,128)(2,1)} %bitcast.342) | data formatting | bytes 25165824 | tf_op jit(solution)/shard_map/convert_element_type | solution.py:19
  326.6 6.9 bitcast_reduce_fusion
  333.5 7.2 fusion.1
  340.6 3.2 copy-done.1
  343.8 16.6 %fusion.5 = f32[1024,1024]{0,1:T(8,128)} fusion(bf16[1024,16,256]{2,1,0:T(8,128)(2,1)S(1)} %bitcast.345), kind=kOutput, calls=%fused_computation.15 | convolution fusion | flops 8589934592 | bytes 12582912 | tf_op jit(solution)/shard_map/dot_general | solution.py:24
  360.7 318.0 %all-reduce.5.cloned.1.call-done = f32[1024,1024]{0,1:T(8,128)} async-done(((f32[1024,1024]{0,1:T(8,128)}), f32[1024,1024]{0,1:T(8,128)}) %all-reduce.5.cloned.1.call-update) | async-done | bytes 4194320 | tf_op jit(solution)/shard_map/psum | solution.py:25
  680.1 12.2 copy.98
  692.4 169.4 %all-reduce.7.cloned.1.call-done = f32[1024,1024]{0,1:T(8,128)} async-done(((f32[1024,1024]{0,1:T(8,128)}), f32[1024,1024]{0,1:T(8,128)}) %all-reduce.7.cloned.1.call-update) | async-done | bytes 4194320 | tf_op jit(solution)/shard_map/psum | solution.py:25
  861.8 2.9 select_reduce_fusion
  865.3 4.8 select_add_fusion
  870.1 5.7 copy.70
  875.9 4.5 fusion.4
  882.3 11.7 cholesky.222
  894.1 9.8 custom-call.64
  907.0 11.7 cholesky.243
  919.3 2.5 cholesky.254
  921.8 9.8 custom-call.65
  934.4 2.7 convolution_subtract_fusion.1
  937.1 11.7 cholesky.466
  949.6 9.8 custom-call.66
  960.7 3.3 convolution_subtract_fusion.2
  964.0 11.7 cholesky.485
  976.5 9.8 custom-call.67
  987.5 3.2 convolution_subtract_fusion.3
  990.6 12.1 cholesky.504
  1003.5 9.8 custom-call.68
  1014.4 3.1 convolution_subtract_fusion.4
  1017.5 11.7 cholesky.524
  1030.0 9.8 custom-call.69
  1040.8 2.8 convolution_subtract_fusion.5
  1043.7 11.7 cholesky.544
  1056.2 9.8 custom-call.70
  1069.0 11.7 cholesky.562
  1090.9 4.9 select_select_fusion
  1095.8 24.5 %while.1 = (s32[]{:T(128)}, f32[1024,1024]{0,1:T(8,128)}, s32[8,2]{0,1:T(2,128)S(1)}, f32[8,128,128]{2,1,0:T(8,128)S(1)}, s32[]{:T(128)}) while((s32[]{:T(128)}, f32[1024,1024]{0,1:T(8,128)}, s32[8,2]{0,1:T(2,128)S(1)}, f32[8,128,128]{2,1,0:T(8,128)S(1)}, s32[]{:T(128)}) %tuple.54), condition=%wide.while_cond, body=%wide.while_body.sunk | while | flops 2 | bytes 393321 | solution.py:29
  1096.4 2.3 dynamic-slice.8
  1099.5 2.3 dynamic-slice.8
  1102.6 2.3 dynamic-slice.8
  1105.6 2.3 dynamic-slice.8
  1108.7 2.3 dynamic-slice.8
  1120.2 78.8 %custom-call.71 = f32[8,128,128]{1,2,0:T(8,128)S(1)} custom-call(f32[8,128,128]{2,1,0:T(8,128)S(1)} %get-tuple-element.16), custom_call_target="InvertDiagBlocksLowerTriangular" | custom-call | tf_op jit(solution)/shard_map/triangular_solve | solution.py:29
  1220.2 2.3 fusion.125
  1223.8 5.7 fusion.126
  (156 shorter events, 63.3 us)
Async XLA Ops:
  6.5 672.1 %all-reduce.5.cloned.1.call-start = ((), (), s32[]{:S(2)}) async-start(), calls=%async_computation.1 | async-start | bytes 8388608 | tf_op jit(solution)/shard_map/psum | solution.py:25
  340.6 3.2 copy-start.1
  360.4 501.4 %all-reduce.7.cloned.1.call-start = ((), (), s32[]{:S(2)}) async-start(), calls=%async_computation.2 | async-start | bytes 8388608 | tf_op jit(solution)/shard_map/psum | solution.py:25
  880.3 2.0 copy-start.2
  1199.1 21.1 %copy-start = (f32[1024,1024]{0,1:T(8,128)S(1)}, f32[1024,1024]{0,1:T(8,128)}, u32[]{:S(2)}) copy-start(f32[1024,1024]{0,1:T(8,128)} %all-reduce.7.cloned.1.call-done) | copy-start | bytes 12582916
Sparse Core Ops, SparseCore 0:
  360.6 318.0 all-reduce.4
  681.2 180.5 all-reduce.6
